TPU v7x, 768 devices: a whole 4x8x12 slice. The times are simulated.
768 devices in a mesh: sample: 32 (over y, z_hi, core), slab: 24 (over z_lo, x).
Axes of the slice: x: 4, y: 8, z: 12 (z_hi: 2, z_lo: 6; z = z_hi * 6 + z_lo), core: 2. Of those that a mesh axis runs over, the one named last changes fastest.
Arguments:
- volumes: bfloat16 [32, 48, 16, 32, 128], P('sample', 'slab'), may hold values from -6 to 6
- kernel: bfloat16 [3, 3, 3, 128, 256], replicated, may hold values from -0.109375 to 0.109375
- cotangent: bfloat16 [32, 24, 8, 16, 256], P('sample', 'slab'), may hold values from -6 to 6
Outputs:
- activations: bfloat16 [32, 24, 8, 16, 256], P('sample', 'slab')
- input_grads: bfloat16 [32, 48, 16, 32, 128], P('sample', 'slab')
- weight_grad: float32 [3456, 256], P('slab', 'sample')
All inputs are finite; a program needn't handle non-finite values.
Results may differ from a plain program's by a relative error of at most 0.0049.
Values may be sent and summed in bfloat16 or wider, within the bound.
No kernel may reach another device: no remote copies, remote signals or barrier semaphores. Data moves between devices by JAX's collectives and lax.ppermute only.
A program may use at most 32 MiB of HBM per device.

v0:
```python
import math

import jax
import jax.numpy as jnp
from jax import lax
from jax.sharding import PartitionSpec as P


def shifted(block, axis, distance):
    devices = range(lax.axis_size(axis))
    route = [(i - distance, i) for i in devices if i - distance in devices]
    return lax.ppermute(block, axis, route)


def activate(values):
    return 0.3 * values + 0.7 * values * jax.nn.sigmoid(values)


def slope_of(values):
    sigmoid_val = jax.nn.sigmoid(values)
    return 0.3 + 0.7 * (sigmoid_val + values * sigmoid_val * (1.0 - sigmoid_val))


def extract_taps(padded, out_depth, out_rows, out_cols):
    leading = padded.shape[0]
    channels = padded.shape[4]
    tap_list = []
    for depth_tap in range(3):
        for row_tap in range(3):
            for col_tap in range(3):
                tap_list.append(
                    lax.slice(
                        padded,
                        (0, depth_tap, row_tap, col_tap, 0),
                        (
                            leading,
                            depth_tap + 2 * out_depth - 1,
                            row_tap + 2 * out_rows - 1,
                            col_tap + 2 * out_cols - 1,
                            channels,
                        ),
                        (1, 2, 2, 2, 1),
                    )
                )
    return jnp.stack(tap_list, axis=4).reshape(-1, 27 * channels)


def fold_taps(source, dim_index, target_len):
    tap_low = lax.index_in_dim(source, 0, 4, keepdims=False)
    tap_mid = lax.index_in_dim(source, 1, 4, keepdims=False)
    tap_high = lax.index_in_dim(source, 2, 4, keepdims=False)
    span_len = tap_low.shape[dim_index]

    def widen(segment, pad_low, pad_high):
        widths_pad = [(0, 0)] * segment.ndim
        widths_pad[dim_index] = (pad_low, pad_high)
        return jnp.pad(segment, widths_pad)

    even_part = widen(tap_low, 0, 1) + widen(tap_high, 1, 0)
    odd_part = widen(tap_mid, 0, 1)
    paired = jnp.stack([even_part, odd_part], axis=dim_index + 1)
    new_shape = list(even_part.shape)
    new_shape[dim_index] = 2 * (span_len + 1)
    return lax.slice_in_dim(paired.reshape(new_shape), 0, target_len, axis=dim_index)


def local(volumes, kernel, cotangent):
    batch_rows, slab_len, height_len, width_len, in_chans = volumes.shape
    out_chans = kernel.shape[-1]
    out_depth = slab_len // 2
    out_rows = height_len // 2
    out_cols = width_len // 2
    weight_rows = kernel.reshape(27 * in_chans, out_chans)
    below_layer = shifted(volumes[:, slab_len - 1 :], "slab", 1)
    extended = jnp.concatenate([below_layer, volumes], axis=1)
    padded = jnp.pad(extended, ((0, 0), (0, 0), (1, 1), (1, 1), (0, 0)))
    patches = extract_taps(padded, out_depth, out_rows, out_cols)
    pre_act = jnp.dot(patches, weight_rows, preferred_element_type=jnp.float32)
    activation = activate(pre_act).astype(jnp.bfloat16)
    out_grad = (cotangent.reshape(-1, out_chans).astype(jnp.float32) * slope_of(pre_act)).astype(
        jnp.bfloat16
    )
    patch_grad = lax.dot_general(
        out_grad, weight_rows, (((1,), (1,)), ((), ())), preferred_element_type=jnp.float32
    )
    shaped = patch_grad.reshape(batch_rows, out_depth, out_rows, out_cols, 3, 3, 3, in_chans)
    shaped = fold_taps(shaped, 1, slab_len + 1)
    shaped = fold_taps(shaped, 2, height_len + 2)
    full_grad = fold_taps(shaped, 3, width_len + 2)
    interior = full_grad[:, 1:, 1 : height_len + 1, 1 : width_len + 1]
    rim_layer = full_grad[:, 0:1, 1 : height_len + 1, 1 : width_len + 1]
    from_next = shifted(rim_layer, "slab", -1)
    input_grad = jnp.concatenate(
        [interior[:, : slab_len - 1], interior[:, slab_len - 1 :] + from_next], axis=1
    ).astype(jnp.bfloat16)
    local_grad = lax.dot_general(
        patches, out_grad, (((0,), (0,)), ((), ())), preferred_element_type=jnp.float32
    )
    column_part = lax.psum_scatter(local_grad, "sample", scatter_dimension=1, tiled=True)
    grad_shard = lax.psum_scatter(column_part, "slab", scatter_dimension=0, tiled=True)
    total_cells = (
        lax.axis_size("sample")
        * batch_rows
        * lax.axis_size("slab")
        * out_depth
        * out_rows
        * out_cols
    )
    norm_factor = 1.0 / math.sqrt(total_cells)
    activations = activation.reshape(batch_rows, out_depth, out_rows, out_cols, out_chans)
    return (activations, input_grad, grad_shard * norm_factor)


def solution(mesh):
    in_specs = (P("sample", "slab", None, None, None), P(), P("sample", "slab", None, None, None))
    out_specs = (
        P("sample", "slab", None, None, None),
        P("sample", "slab", None, None, None),
        P("slab", "sample"),
    )
    return jax.shard_map(local, mesh=mesh, in_specs=in_specs, out_specs=out_specs, check_vma=False)
```

profile of v0, /device:TPU:16, one launch (start us, length us, event | category | flops | bytes accessed | tf_op | source)
XLA Modules:
  0.0 708.5 jit_solution(7487228023065980637)
XLA Ops:
  7.2 1.0 slice.155
  8.3 3.4 collective-permute-start
  11.7 2.7 collective-permute-done
  14.4 1.1 fusion.17
  21.8 0.6 copy.37
  22.5 1.1 fusion.20
  23.6 2.5 fusion.8
  26.2 1.3 dynamic-slice
  28.1 0.7 fusion.2
  29.2 0.2 pad_maximum_fusion
  29.4 0.2 copy.40
  30.7 1.0 copy.46
  31.7 0.7 slice.206
  32.4 0.3 slice.220
  32.7 1.3 collective-permute-start.1
  34.0 475.7 %all-reduce.13.cloned.1.call-done = f32[3456,256]{0,1:T(8,128)} async-done(((f32[3456,256]{0,1:T(8,128)}), f32[3456,256]{0,1:T(8,128)}) %all-reduce.13.cloned.1.call-update) | async-done | bytes 3538960
  509.7 0.9 constant_dynamic-slice_fusion
  510.6 1.8 copy.49
  512.4 0.3 fusion.19
  512.7 0.9 pad_maximum_fusion.3
  513.6 0.7 copy.47
  514.3 185.8 %reduce-scatter.4.cloned.1.call-done = f32[144,8]{1,0:T(8,128)} async-done(((f32[3456,8]{1,0:T(8,128)}), f32[144,8]{1,0:T(8,128)}) %reduce-scatter.4.cloned.1.call-update) | async-done | bytes 4624
  700.1 0.9 copy.50
  701.0 0.6 broadcast_multiply_fusion
  (74 shorter events, 7.5 us)
Async XLA Ops:
  7.2 15.2 %copy-start = (bf16[3,3,3,128,256]{4,3,2,1,0:T(8,128)(2,1)S(1)}, bf16[3,3,3,128,256]{4,3,2,1,0:T(8,128)(2,1)}, u32[]{:S(2)}) copy-start(bf16[3,3,3,128,256]{4,3,2,1,0:T(8,128)(2,1)} %param.4) | copy-start | bytes 5308420
  7.2 502.5 %all-reduce.13.cloned.1.call-start = ((), (), s32[]{:S(2)}) async-start(), calls=%async_computation.2 | async-start | bytes 7077888
  8.3 6.1 collective-permute-start
  21.6 0.8 copy-start.1
  26.1 674.0 %reduce-scatter.4.cloned.1.call-start = ((), (), s32[]{:S(2)}) async-start(), calls=%async_computation.1 | async-start | bytes 1843200
  32.7 479.7 %collective-permute-start.1 = (f32[1,1,16,32,128]{4,0,3,2,1:T(1,128)}, f32[1,1,16,32,128]{4,0,3,2,1:T(1,128)S(1)}, u32[]{:S(2)}, u32[]{:S(2)}) collective-permute-start(f32[1,1,16,32,128]{4,0,3,2,1:T(1,128)} %slice.206), channel_id=1, source_target_pairs={{1,0},{2,1},{3,2},{4,3},{5,4},{6,5},{7,6},{8,7},{9,8},{10,9},{11,1... | collective-permute-start | bytes 786440 | tf_op jit(solution)/shard_map/ppermute | solution.py:12
Sparse Core Ops, SparseCore 0:
  26.2 483.4 all-reduce.12
  512.8 187.2 reduce-scatter.3
where the time goes:
time: 709 us
  waiting for transfers between devices  664 us (94%)
  local copies, waits for them, and re-layouts  16.2 us (2%)
  between operations  15.2 us (2%)
    unnamed x4, waiting for transfers between devices  662 us
  transfers between devices with their start and end apart: 4, of which 3 were waited for; matrix products, arithmetic and copies ran while one was open for 1% of the time, Pallas kernels for 0%

commit v1 on v0

--- a/solution.py
+++ b/solution.py
@@ -3,13 +3,17 @@
 import jax
 import jax.numpy as jnp
 from jax import lax
-from jax.sharding import PartitionSpec as P
+from jax.sharding import Mesh, PartitionSpec as P
+
+Y, ZH, CORE, ZL, X = 8, 2, 2, 6, 4
+AXES = ("y", "zh", "core", "zl", "x")
+SLAB = ("zl", "x")
 
 
-def shifted(block, axis, distance):
-    devices = range(lax.axis_size(axis))
+def shifted(block, distance):
+    devices = range(ZL * X)
     route = [(i - distance, i) for i in devices if i - distance in devices]
-    return lax.ppermute(block, axis, route)
+    return lax.ppermute(block, SLAB, route)
 
 
 def activate(values):
@@ -64,6 +68,33 @@
     return lax.slice_in_dim(paired.reshape(new_shape), 0, target_len, axis=dim_index)
 
 
+def exchange(block, axes):
+    return lax.all_to_all(block, axes, 0, 0, tiled=True)
+
+
+def total(parts):
+    return jnp.sum(parts.astype(jnp.float32), axis=0)
+
+
+def reduce_weights(patches, out_grad, out_chans):
+    wanted = jnp.arange(out_chans).reshape(Y, ZH, CORE, -1).transpose(2, 0, 1, 3).reshape(-1)
+    choose = (jnp.arange(out_chans)[:, None] == wanted[None, :]).astype(jnp.bfloat16)
+    reordered = jnp.dot(out_grad, choose, preferred_element_type=jnp.float32).astype(jnp.bfloat16)
+    grad = lax.dot_general(
+        patches, reordered, (((0,), (0,)), ((), ())), preferred_element_type=jnp.float32
+    ).astype(jnp.bfloat16)
+    rows = grad.shape[0] // (ZL * X)
+    half = out_chans // CORE
+    grad = grad.reshape(ZL, X, rows, CORE, half).transpose(3, 1, 0, 2, 4)
+    grad = total(exchange(grad, "core")[:CORE]).astype(jnp.bfloat16)
+    grad = total(exchange(grad, "x")).astype(jnp.bfloat16)
+    grad = grad.reshape(ZL * rows, half).T.reshape(Y, half // Y, ZL * rows)
+    grad = total(exchange(grad, "y"))
+    filters = half // Y // ZH
+    grad = grad.reshape(ZH, filters, ZL, rows).transpose(0, 2, 1, 3).reshape(ZH * ZL, filters, rows)
+    return total(exchange(grad, ("zh", "zl"))).T
+
+
 def local(volumes, kernel, cotangent):
     batch_rows, slab_len, height_len, width_len, in_chans = volumes.shape
     out_chans = kernel.shape[-1]
@@ -71,7 +102,7 @@
     out_rows = height_len // 2
     out_cols = width_len // 2
     weight_rows = kernel.reshape(27 * in_chans, out_chans)
-    below_layer = shifted(volumes[:, slab_len - 1 :], "slab", 1)
+    below_layer = shifted(volumes[:, slab_len - 1 :], 1)
     extended = jnp.concatenate([below_layer, volumes], axis=1)
     padded = jnp.pad(extended, ((0, 0), (0, 0), (1, 1), (1, 1), (0, 0)))
     patches = extract_taps(padded, out_depth, out_rows, out_cols)
@@ -89,33 +120,19 @@
     full_grad = fold_taps(shaped, 3, width_len + 2)
     interior = full_grad[:, 1:, 1 : height_len + 1, 1 : width_len + 1]
     rim_layer = full_grad[:, 0:1, 1 : height_len + 1, 1 : width_len + 1]
-    from_next = shifted(rim_layer, "slab", -1)
+    from_next = shifted(rim_layer, -1)
     input_grad = jnp.concatenate(
         [interior[:, : slab_len - 1], interior[:, slab_len - 1 :] + from_next], axis=1
     ).astype(jnp.bfloat16)
-    local_grad = lax.dot_general(
-        patches, out_grad, (((0,), (0,)), ((), ())), preferred_element_type=jnp.float32
-    )
-    column_part = lax.psum_scatter(local_grad, "sample", scatter_dimension=1, tiled=True)
-    grad_shard = lax.psum_scatter(column_part, "slab", scatter_dimension=0, tiled=True)
-    total_cells = (
-        lax.axis_size("sample")
-        * batch_rows
-        * lax.axis_size("slab")
-        * out_depth
-        * out_rows
-        * out_cols
-    )
+    grad_shard = reduce_weights(patches, out_grad, out_chans)
+    total_cells = Y * ZH * CORE * batch_rows * ZL * X * out_depth * out_rows * out_cols
     norm_factor = 1.0 / math.sqrt(total_cells)
     activations = activation.reshape(batch_rows, out_depth, out_rows, out_cols, out_chans)
     return (activations, input_grad, grad_shard * norm_factor)
 
 
 def solution(mesh):
-    in_specs = (P("sample", "slab", None, None, None), P(), P("sample", "slab", None, None, None))
-    out_specs = (
-        P("sample", "slab", None, None, None),
-        P("sample", "slab", None, None, None),
-        P("slab", "sample"),
-    )
-    return jax.shard_map(local, mesh=mesh, in_specs=in_specs, out_specs=out_specs, check_vma=False)
+    fine = Mesh(mesh.devices.reshape(Y, ZH, CORE, ZL, X), AXES)
+    split = P(("y", "zh", "core"), SLAB, None, None, None)
+    out_specs = (split, split, P(SLAB, ("y", "zh", "core")))
+    return jax.shard_map(local, mesh=fine, in_specs=(split, P(), split), out_specs=out_specs, check_vma=False)

time: 709 us -> 98.8 us (0.14)
  the two profiles are of different devices: /device:TPU:16 before, /device:TPU:2 now
where the time goes in v1:
time: 98.8 us; the launch traced here: 98.1 us
  waiting for transfers between devices  31.3 us (32%)
  starting transfers between devices  29.1 us (29%)
  local copies, waits for them, and re-layouts  19.8 us (20%)
  other arithmetic  7.49 us (8%)
  blocking collectives  5.16 us (5%)
  matrix products  3.94 us (4%)
  between operations  1.23 us (1%)
    all_to_all x3, starting transfers between devices, exchange(): return lax.all_to_all(block, axes, 0, 0, tiled=True)  22.4 us
    all_to_all x3, waiting for transfers between devices, exchange(): return lax.all_to_all(block, axes, 0, 0, tiled=True)  21.1 us
    ppermute x2, waiting for transfers between devices, shifted(): return lax.ppermute(block, SLAB, route)  10.2 us
    ppermute x2, starting transfers between devices, shifted(): return lax.ppermute(block, SLAB, route)  6.76 us
    slice x27, local copies, waits for them, and re-layouts, extract_taps(): lax.slice(padded, (0, depth_tap, row_tap, col_tap, 0), (leading, depth_ta...  5.63 us
    all_to_all x1, blocking collectives, exchange(): return lax.all_to_all(block, axes, 0, 0, tiled=True)  5.16 us
    reshape x2, local copies, waits for them, and re-layouts, reduce_weights(): grad = grad.reshape(ZL, X, rows, CORE, half).transpose(3, 1, 0, 2, 4)  3.76 us
    reduce_sum x1, local copies, waits for them, and re-layouts, total(): return jnp.sum(parts.astype(jnp.float32), axis=0)  2.14 us
  transfers between devices with their start and end apart: 5, of which 4 were waited for; matrix products, arithmetic and copies ran while one was open for 10% of the time, Pallas kernels for 0%

profile of v1, /device:TPU:2, one launch (start us, length us, event | category | flops | bytes accessed | tf_op | source)
XLA Modules:
  0.0 98.1 jit_solution(16633790738705077743)
XLA Ops:
  0.6 1.0 %slice.155 = bf16[1,1,16,32,128]{4,3,2,1,0:T(8,128)(2,1)S(1)} slice(bf16[1,2,16,32,128]{4,3,2,1,0:T(8,128)(2,1)} %param.3), slice={[0:1], [1:2], [0:16], [0:32], [0:128]} | slice | bytes 262144 | tf_op jit(solution)/shard_map/slice | solution.py:105
  1.7 3.4 %collective-permute-start = (bf16[1,1,16,32,128]{4,3,2,1,0:T(8,128)(2,1)S(1)}, bf16[1,1,16,32,128]{4,3,2,1,0:T(8,128)(2,1)S(1)}, u32[]{:S(2)}, u32[]{:S(2)}) collective-permute-start(bf16[1,1,16,32,128]{4,3,2,1,0:T(8,128)(2,1)S(1)} %slice.155), channel_id=1, source_target_pairs={{0,1},{1,2},{2,3},{3,4},{4,5},{5,6},{6,7},{7,8},{8,9},{9,10},{10,1... | collective-permute-start | bytes 393224 | tf_op jit(solution)/shard_map/ppermute | solution.py:16
  5.2 10.2 %collective-permute-done = bf16[1,1,16,32,128]{4,3,2,1,0:T(8,128)(2,1)S(1)} collective-permute-done((bf16[1,1,16,32,128]{4,3,2,1,0:T(8,128)(2,1)S(1)}, bf16[1,1,16,32,128]{4,3,2,1,0:T(8,128)(2,1)S(1)}, u32[]{:S(2)}, u32[]{:S(2)}) %collective-permute-start) | collective-permute-done | bytes 131104 | tf_op jit(solution)/shard_map/ppermute | solution.py:16
  15.4 1.1 %fusion.16 = bf16[1,3,18,34,128]{4,3,2,1,0:T(8,128)(2,1)S(1)} fusion(bf16[1,2,16,32,128]{4,3,2,1,0:T(8,128)(2,1)} %param.3, bf16[1,1,16,32,128]{4,3,2,1,0:T(8,128)(2,1)S(1)} %collective-permute-done), kind=kLoop, calls=%fused_computation.36 | loop fusion | flops 3525120 | bytes 863232 | tf_op jit(solution)/shard_map/concatenate | solution.py:106
  23.5 1.2 %fusion.19 = (bf16[128,256]{1,0:T(8,128)(2,1)}, bf16[128,256]{1,0:T(8,128)(2,1)}) fusion(bf16[1,1,8,16,256]{4,3,2,1,0:T(8,128)(2,1)S(1)} %copy-done.3, bf16[3456,256]{1,0:T(8,128)(2,1)S(1)} %bitcast.139, bf16[16,8,27,128]{3,2,1,0:T(8,128)(2,1)S(1)} %bitcast.143), kind=kOutput, calls=%fused_computation.48 | convolution fusion | flops 227049472 | bytes 2850816 | tf_op jit(solution)/shard_map/dot_general | solution.py:109
  24.7 2.1 %convolution_convert_fusion = bf16[3456,256]{1,0:T(8,128)(2,1)S(1)} fusion(bf16[128,256]{1,0:T(8,128)(2,1)} %get-tuple-element.21, bf16[16,8,27,128]{3,2,1,0:T(8,128)(2,1)} %bitcast.144, s32[256]{0:T(256)S(1)} %reshape.155), kind=kOutput, calls=%fused_computation | convolution fusion | flops 244252672 | bytes 2720768 | tf_op jit(solution)/shard_map/dot_general | solution.py:83
  26.8 2.0 %reshape.156 = bf16[6,4,144,2,128]{4,3,2,1,0:T(2,128)(2,1)} reshape(bf16[3456,256]{1,0:T(8,128)(2,1)S(1)} %convolution_convert_fusion) | data formatting | bytes 3538944 | tf_op jit(solution)/shard_map/reshape | solution.py:88
  28.7 1.8 %copy.93 = bf16[6,4,144,2,128]{4,2,1,0,3:T(8,128)(2,1)S(1)} copy(bf16[6,4,144,2,128]{4,3,2,1,0:T(2,128)(2,1)} %reshape.156) | data formatting | bytes 3538944 | tf_op jit(solution)/shard_map/reshape | solution.py:88
  30.5 5.2 %all_to_all.20 = bf16[2,4,6,144,128]{4,3,1,2,0:T(8,128)(2,1)S(1)} all-to-all(bf16[2,4,6,144,128]{4,3,1,2,0:T(8,128)(2,1)S(1)} %bitcast.141), channel_id=1, replica_groups=mesh['y'=8,'zh'=2,'core'=2,'zl'=6,'x'=4] {'core'}, dimensions={0} | all-to-all | bytes 3538944 | tf_op jit(solution)/shard_map/all_to_all | solution.py:72
  35.7 1.5 %reduce_sum.42 = bf16[4,6,144,128]{3,2,0,1:T(8,128)(2,1)} reduce(bf16[2,4,6,144,128]{4,3,1,2,0:T(8,128)(2,1)S(1)} %all_to_all.20, bf16[]{:T(256)} %constant.13.clone.1), dimensions={0}, to_apply=%region_0.1 | reduce | flops 442368 | bytes 2654210 | tf_op jit(solution)/shard_map/reduce_sum | solution.py:76
  37.2 2.1 %copy.69 = bf16[4,6,144,128]{3,2,1,0:T(8,128)(2,1)} copy(bf16[4,6,144,128]{3,2,0,1:T(8,128)(2,1)} %reduce_sum.42) | data formatting | bytes 1769472 | tf_op jit(solution)/shard_map/reduce_sum | solution.py:76
  39.3 3.6 %all-to-all-start.1 = ((bf16[4,6,144,128]{3,2,1,0:T(8,128)(2,1)}), bf16[4,6,144,128]{3,2,1,0:T(8,128)(2,1)S(1)}, u32[]{:S(2)}, u32[]{:S(2)}) async-start(bf16[4,6,144,128]{3,2,1,0:T(8,128)(2,1)} %copy.69), calls=%async_computation.1 | async-start | bytes 1769472 | tf_op jit(solution)/shard_map/all_to_all | solution.py:72
  45.1 1.1 %slice_bitcast_fusion.8 = (f32[1,3,18,16,128]{4,3,2,1,0:T(8,128)}, f32[1,3,18,16,128]{4,3,2,1,0:T(8,128)S(1)}, f32[1,3,18,16,128]{4,3,2,1,0:T(8,128)}) fusion(f32[1,3,18,16,3,128]{5,3,4,2,1,0:T(8,128)S(1)} %bitcast.142), kind=kLoop, calls=%fused_computation.42 | loop fusion | bytes 2654208 | tf_op jit(solution)/shard_map/squeeze | solution.py:53
  46.3 8.7 %all-to-all-done.1 = bf16[4,6,144,128]{3,2,1,0:T(8,128)(2,1)S(1)} async-done(((bf16[4,6,144,128]{3,2,1,0:T(8,128)(2,1)}), bf16[4,6,144,128]{3,2,1,0:T(8,128)(2,1)S(1)}, u32[]{:S(2)}, u32[]{:S(2)}) %all-to-all-start.1) | async-done | bytes 884768 | tf_op jit(solution)/shard_map/all_to_all | solution.py:72
  55.1 0.8 copy.70
  56.0 3.4 %all-to-all-start.2 = ((bf16[8,16,864]{2,1,0:T(8,128)(2,1)}), bf16[8,16,864]{2,1,0:T(8,128)(2,1)S(1)}, u32[]{:S(2)}, u32[]{:S(2)}) async-start(bf16[8,16,864]{2,1,0:T(8,128)(2,1)} %bitcast.56), calls=%async_computation.2 | async-start | bytes 458752 | tf_op jit(solution)/shard_map/all_to_all | solution.py:72
  59.4 1.2 %add_bitcast_fusion.1 = f32[1,3,18,17,1,128]{5,3,2,1,4,0:T(8,128)S(1)} fusion(f32[1,3,18,16,128]{4,3,2,1,0:T(8,128)} %get-tuple-element.20, f32[1,3,18,16,128]{4,3,2,1,0:T(8,128)} %get-tuple-element.18), kind=kLoop, calls=%fused_computation.24 | loop fusion | flops 117504 | bytes 1354752 | tf_op jit(solution)/shard_map/stack | solution.py:65
  60.7 1.0 copy.66
  62.4 3.4 %collective-permute-start.1 = (f32[1,1,16,32,128]{4,0,3,2,1:T(1,128)}, f32[1,1,16,32,128]{4,0,3,2,1:T(1,128)}, u32[]{:S(2)}, u32[]{:S(2)}) collective-permute-start(f32[1,1,16,32,128]{4,0,3,2,1:T(1,128)} %slice.206), channel_id=1, source_target_pairs={{1,0},{2,1},{3,2},{4,3},{5,4},{6,5},{7,6},{8,7},{9,8},{10,9},{11,1... | collective-permute-start | bytes 786440 | tf_op jit(solution)/shard_map/ppermute | solution.py:16
  66.0 3.9 %all-to-all-done.2 = bf16[8,16,864]{2,1,0:T(8,128)(2,1)S(1)} async-done(((bf16[8,16,864]{2,1,0:T(8,128)(2,1)}), bf16[8,16,864]{2,1,0:T(8,128)(2,1)S(1)}, u32[]{:S(2)}, u32[]{:S(2)}) %all-to-all-start.2) | async-done | bytes 221216 | tf_op jit(solution)/shard_map/all_to_all | solution.py:72
  70.8 15.4 %all-to-all-start.3 = ((f32[12,8,144]{2,1,0:T(8,128)}), f32[12,8,144]{2,1,0:T(8,128)S(1)}, u32[]{:S(2)}, u32[]{:S(2)}) async-start(f32[12,8,144]{2,1,0:T(8,128)} %bitcast.58), calls=%async_computation.3 | async-start | bytes 196608 | tf_op jit(solution)/shard_map/all_to_all | solution.py:72
  86.1 1.2 %fusion.18 = bf16[1,1,16,32,128]{4,0,3,2,1:T(2,128)(2,1)S(1)} fusion(f32[1,1,16,32,128]{4,0,3,2,1:T(1,128)} %collective-permute-done.1, f32[1,3,18,34,128]{4,0,3,2,1:T(1,128)S(1)} %bitcast.147), kind=kLoop, calls=%fused_computation.44 | loop fusion | flops 131072 | bytes 655360 | tf_op jit(solution)/shard_map/convert.4
  87.4 0.9 pad_maximum_fusion.3
  89.0 8.5 %all-to-all-done.3 = f32[12,8,144]{2,1,0:T(8,128)S(1)} async-done(((f32[12,8,144]{2,1,0:T(8,128)}), f32[12,8,144]{2,1,0:T(8,128)S(1)}, u32[]{:S(2)}, u32[]{:S(2)}) %all-to-all-start.3) | async-done | bytes 55328 | tf_op jit(solution)/shard_map/all_to_all | solution.py:72
  (87 shorter events, 12.3 us)
Async XLA Ops:
  0.6 22.8 %copy-start = (bf16[3,3,3,128,256]{4,3,2,1,0:T(8,128)(2,1)S(1)}, bf16[3,3,3,128,256]{4,3,2,1,0:T(8,128)(2,1)}, u32[]{:S(2)}) copy-start(bf16[3,3,3,128,256]{4,3,2,1,0:T(8,128)(2,1)} %param.4) | copy-start | bytes 5308420
  1.7 13.7 %collective-permute-start = (bf16[1,1,16,32,128]{4,3,2,1,0:T(8,128)(2,1)S(1)}, bf16[1,1,16,32,128]{4,3,2,1,0:T(8,128)(2,1)S(1)}, u32[]{:S(2)}, u32[]{:S(2)}) collective-permute-start(bf16[1,1,16,32,128]{4,3,2,1,0:T(8,128)(2,1)S(1)} %slice.155), channel_id=1, source_target_pairs={{0,1},{1,2},{2,3},{3,4},{4,5},{5,6},{6,7},{7,8},{8,9},{9,10},{10,1... | collective-permute-start | bytes 393224 | tf_op jit(solution)/shard_map/ppermute | solution.py:16
  22.7 0.8 copy-start.3
  23.5 1.2 %copy-start.1 = (bf16[1,1,8,16,27,128]{5,4,3,2,1,0:T(8,128)(2,1)}, bf16[1,1,8,16,27,128]{5,4,3,2,1,0:T(8,128)(2,1)S(1)}, u32[]{:S(2)}) copy-start(bf16[1,1,8,16,27,128]{5,4,3,2,1,0:T(8,128)(2,1)S(1)} %copy.57) | copy-start | bytes 2654212
  39.3 3.6 %copy-start.2 = (bf16[128,256]{1,0:T(8,128)(2,1)S(1)}, bf16[128,256]{1,0:T(8,128)(2,1)}, u32[]{:S(2)}) copy-start(bf16[128,256]{1,0:T(8,128)(2,1)} %get-tuple-element.21) | copy-start | bytes 196612
  39.3 15.6 %all-to-all-start.1 = ((bf16[4,6,144,128]{3,2,1,0:T(8,128)(2,1)}), bf16[4,6,144,128]{3,2,1,0:T(8,128)(2,1)S(1)}, u32[]{:S(2)}, u32[]{:S(2)}) async-start(bf16[4,6,144,128]{3,2,1,0:T(8,128)(2,1)} %copy.69), calls=%async_computation.1 | async-start | bytes 1769472 | tf_op jit(solution)/shard_map/all_to_all | solution.py:72
  56.0 14.0 %all-to-all-start.2 = ((bf16[8,16,864]{2,1,0:T(8,128)(2,1)}), bf16[8,16,864]{2,1,0:T(8,128)(2,1)S(1)}, u32[]{:S(2)}, u32[]{:S(2)}) async-start(bf16[8,16,864]{2,1,0:T(8,128)(2,1)} %bitcast.56), calls=%async_computation.2 | async-start | bytes 458752 | tf_op jit(solution)/shard_map/all_to_all | solution.py:72
  62.4 23.7 %collective-permute-start.1 = (f32[1,1,16,32,128]{4,0,3,2,1:T(1,128)}, f32[1,1,16,32,128]{4,0,3,2,1:T(1,128)}, u32[]{:S(2)}, u32[]{:S(2)}) collective-permute-start(f32[1,1,16,32,128]{4,0,3,2,1:T(1,128)} %slice.206), channel_id=1, source_target_pairs={{1,0},{2,1},{3,2},{4,3},{5,4},{6,5},{7,6},{8,7},{9,8},{10,9},{11,1... | collective-permute-start | bytes 786440 | tf_op jit(solution)/shard_map/ppermute | solution.py:16
  70.8 26.7 %all-to-all-start.3 = ((f32[12,8,144]{2,1,0:T(8,128)}), f32[12,8,144]{2,1,0:T(8,128)S(1)}, u32[]{:S(2)}, u32[]{:S(2)}) async-start(f32[12,8,144]{2,1,0:T(8,128)} %bitcast.58), calls=%async_computation.3 | async-start | bytes 196608 | tf_op jit(solution)/shard_map/all_to_all | solution.py:72

commit v2 on v1

v2 whole, which is shorter than its diff:
```python
import math

import jax
import jax.numpy as jnp
from jax import lax
from jax.experimental import pallas as pl
from jax.experimental.pallas import tpu as pltpu
from jax.sharding import Mesh, PartitionSpec as P

Y, ZH, CORE, ZL, X = 8, 2, 2, 6, 4
AXES = ("y", "zh", "core", "zl", "x")
SLAB = ("zl", "x")
ROWS, COLS = 8, 16
IN, OUT = 128, 256
CELLS = ROWS * COLS
TAPS = [(a, b, c) for a in range(3) for b in range(3) for c in range(3)]
SHARE = 27 * IN // (ZL * X)
HALF = OUT // CORE
PAD = 8
BF, F32 = jnp.bfloat16, jnp.float32
VMEM = pl.BlockSpec(memory_space=pltpu.VMEM)


def shifted(block, distance):
    devices = range(ZL * X)
    route = [(i - distance, i) for i in devices if i - distance in devices]
    return lax.ppermute(block, SLAB, route)


def forward_kernel(own_ref, below_ref, weight_ref, cot_ref, act_ref, grad_ref, dw_ref, wide, patches):
    zero = jnp.zeros((COLS, IN), BF)
    for layer in range(3):
        for h in range(2 * ROWS):
            source = below_ref[h] if layer == 0 else own_ref[layer - 1, h]
            wide[layer, h, 0:PAD, :] = jnp.zeros((PAD, IN), F32)
            wide[layer, h, PAD : PAD + 2 * COLS, :] = source.astype(F32)
    for tap, (a, b, c) in enumerate(TAPS):
        lanes = slice(tap * IN, (tap + 1) * IN)
        for p in range(ROWS):
            h = 2 * p - 1 + b
            if h < 0:
                piece = zero
            else:
                piece = wide[a, h, pl.ds(PAD - 1 + c, COLS, stride=2), :].astype(BF)
            patches[p * COLS : (p + 1) * COLS, lanes] = piece
    pre = jnp.dot(patches[...], weight_ref[...], preferred_element_type=F32)
    sig = jax.nn.sigmoid(pre)
    act_ref[...] = (0.3 * pre + 0.7 * pre * sig).astype(BF)
    slope = 0.3 + 0.7 * (sig + pre * sig * (1.0 - sig))
    grad = (cot_ref[...].astype(F32) * slope).astype(BF)
    grad_ref[...] = grad
    place = lax.broadcasted_iota(jnp.int32, (OUT, OUT), 1)
    origin = lax.broadcasted_iota(jnp.int32, (OUT, OUT), 0)
    wanted = (place % HALF) // 8 * 16 + place // HALF * 8 + place % 8
    choose = jnp.where(origin == wanted, 1.0, 0.0).astype(BF)
    ordered = jnp.dot(grad, choose, preferred_element_type=F32).astype(BF)
    for tap in range(27):
        lanes = slice(tap * IN, (tap + 1) * IN)
        part = lax.dot_general(
            patches[:, lanes], ordered, (((0,), (0,)), ((), ())), preferred_element_type=F32
        ).astype(BF)
        for k in range(IN // 16):
            slab, inner = divmod(tap * (IN // 16) + k, SHARE // 16)
            zl, x = divmod(slab, X)
            for core in range(CORE):
                dw_ref[core, x, zl, inner * 16 : (inner + 1) * 16, :] = part[
                    k * 16 : (k + 1) * 16, core * HALF : (core + 1) * HALF
                ]


def forward(own, below, weights, cotangent):
    return pl.pallas_call(
        forward_kernel,
        out_shape=(
            jax.ShapeDtypeStruct((CELLS, OUT), BF),
            jax.ShapeDtypeStruct((CELLS, OUT), BF),
            jax.ShapeDtypeStruct((CORE, X, ZL, SHARE, HALF), BF),
        ),
        in_specs=[VMEM] * 4,
        out_specs=(VMEM,) * 3,
        scratch_shapes=[
            pltpu.VMEM((3, 2 * ROWS, PAD + 2 * COLS, IN), F32),
            pltpu.VMEM((CELLS, 27 * IN), BF),
        ],
        cost_estimate=pl.CostEstimate(flops=4 * CELLS * 27 * IN * OUT, bytes_accessed=4 << 20, transcendentals=CELLS * OUT),
        name="forward",
    )(own, below, weights, cotangent)


def backward_kernel(grad_ref, next_ref, weight_ref, out_ref, wide):
    def moved(ref):
        grad = ref[...].astype(F32)
        cell = lax.broadcasted_iota(jnp.int32, (CELLS, OUT), 0)
        ahead = jnp.concatenate([grad[1:], jnp.zeros((1, OUT), F32)], axis=0)
        ahead = jnp.where(cell % COLS == COLS - 1, 0.0, ahead)
        blank = jnp.zeros((COLS, OUT), BF)
        found = {}
        for dq, value in ((0, ref[...]), (1, ahead.astype(BF))):
            found[0, dq] = value
            found[1, dq] = jnp.concatenate([value[COLS:], blank], axis=0)
        return found

    mine, after = moved(grad_ref), moved(next_ref)
    choices = {0: [(1, 0)], 1: [(2, 0), (0, 1)]}
    for layer in range(2):
        sources = [(1, mine)] if layer == 0 else [(2, mine), (0, after)]
        for hp in range(2):
            for wp in range(2):
                value = jnp.zeros((CELLS, IN), F32)
                for a, found in sources:
                    for b, dp in choices[hp]:
                        for c, dq in choices[wp]:
                            value += lax.dot_general(
                                found[dp, dq],
                                weight_ref[(a * 3 + b) * 3 + c],
                                (((1,), (1,)), ((), ())),
                                preferred_element_type=F32,
                            )
                for p in range(ROWS):
                    wide[layer, 2 * p + hp, pl.ds(wp, COLS, stride=2), :] = value[p * COLS : (p + 1) * COLS]
    out_ref[...] = wide[...].astype(BF)


def backward(grad, grad_next, weights):
    return pl.pallas_call(
        backward_kernel,
        out_shape=jax.ShapeDtypeStruct((2, 2 * ROWS, 2 * COLS, IN), BF),
        in_specs=[VMEM] * 3,
        out_specs=VMEM,
        scratch_shapes=[pltpu.VMEM((2, 2 * ROWS, 2 * COLS, IN), F32)],
        cost_estimate=pl.CostEstimate(flops=2 * CELLS * 27 * IN * OUT, bytes_accessed=3 << 20, transcendentals=0),
        name="backward",
    )(grad, grad_next, weights)


def exchange(block, axes):
    return lax.all_to_all(block, axes, 0, 0, tiled=True)


def total(parts):
    return jnp.sum(parts.astype(F32), axis=0)


def reduce_weights(grad):
    grad = total(exchange(grad, "core")).astype(BF)
    grad = total(exchange(grad, "x")).astype(BF)
    grad = grad.reshape(ZL * SHARE, HALF).T.reshape(Y, HALF // Y, ZL * SHARE)
    grad = total(exchange(grad, "y"))
    grad = grad.reshape(ZH, 8, ZL, SHARE).transpose(0, 2, 1, 3).reshape(ZH * ZL, 8, SHARE)
    return total(exchange(grad, ("zh", "zl"))).T


def local(volumes, kernel, cotangent):
    own = volumes[0]
    below = shifted(volumes[0, 1], 1)
    activation, out_grad, partial = forward(
        own, below, kernel.reshape(27 * IN, OUT), cotangent.reshape(CELLS, OUT)
    )
    next_grad = shifted(out_grad, -1)
    input_grad = backward(out_grad, next_grad, kernel.reshape(27, IN, OUT))
    grad_shard = reduce_weights(partial)
    norm_factor = 1.0 / math.sqrt(Y * ZH * CORE * ZL * X * CELLS)
    return (
        activation.reshape(1, 1, ROWS, COLS, OUT),
        input_grad[None],
        grad_shard * norm_factor,
    )


def solution(mesh):
    fine = Mesh(mesh.devices.reshape(Y, ZH, CORE, ZL, X), AXES)
    split = P(("y", "zh", "core"), SLAB, None, None, None)
    out_specs = (split, split, P(SLAB, ("y", "zh", "core")))
    return jax.shard_map(local, mesh=fine, in_specs=(split, P(), split), out_specs=out_specs, check_vma=False)
```

time: 98.8 us -> 84.4 us (0.85)
  blocking collectives: 5.16 us -> 34.4 us
  local copies, waits for them, and re-layouts: 19.8 us -> 3.11 us
  waiting for transfers between devices: 31.3 us -> 14.7 us
  Pallas kernels: 0 us -> 7.47 us
  starting transfers between devices: 29.1 us -> 22.2 us
  other arithmetic: 7.49 us -> 1.25 us
  matrix products: 3.94 us -> 0 us
    all_to_all x1 -> x3, blocking collectives: 5.16 us -> 34.4 us  [exchange(): return lax.all_to_all(block, axes, 0, 0, tiled=True)]
    all_to_all x3 -> x1, waiting for transfers between devices: 21.1 us -> 1.6 us  [exchange(): return lax.all_to_all(block, axes, 0, 0, tiled=True)]
    slice x30 -> x0, local copies, waits for them, and re-layouts: 7.68 us -> none  [the longest x27 5.63 us: extract_taps(): lax.slice(padded, (0, depth_tap, row_tap, col_tap, 0), (leading, depth_ta...]
    pallas_call x0 -> x2, Pallas kernels: none -> 7.47 us  [the longest x1 4.53 us: forward(): pl.pallas_call(forward_kernel, out_shape=(jax.ShapeDtypeStruct((CELLS, OU...]
    all_to_all x3 -> x1, starting transfers between devices: 22.4 us -> 15.5 us  [exchange(): return lax.all_to_all(block, axes, 0, 0, tiled=True)]
    dot_general x3 -> x0, matrix products: 3.94 us -> none  [the longest x1 2.07 us: reduce_weights(): lax.dot_general(patches, reordered, (((0,), (0,)), ((), ())), preferred_e...]
    reshape x4 -> x1, local copies, waits for them, and re-layouts: 3.95 us -> 0.1 us  [reduce_weights(): grad.reshape(ZH, 8, ZL, SHARE).transpose(0, 2, 1, 3)]
    another operation x7 -> x0, other arithmetic: 3.18 us -> none  [the longest x6 1.95 us: fold_taps(): paired = jnp.stack([even_part, odd_part], axis=dim_index + 1)]
  transfers between devices with their start and end apart: 5 -> 3, of which waited for: 4 -> 3; matrix products, arithmetic and copies ran while one was open for 10% -> 0% of each run, Pallas kernels for 0% -> 4%
where the time goes in v2:
time: 84.4 us; the launch traced here: 83.9 us
  blocking collectives  34.4 us (41%)
  starting transfers between devices  22.2 us (26%)
  waiting for transfers between devices  14.7 us (17%)
  Pallas kernels  7.47 us (9%)
  local copies, waits for them, and re-layouts  3.11 us (4%)
  other arithmetic  1.25 us (1%)
    all_to_all x3, blocking collectives, exchange(): return lax.all_to_all(block, axes, 0, 0, tiled=True)  34.4 us
    all_to_all x1, starting transfers between devices, exchange(): return lax.all_to_all(block, axes, 0, 0, tiled=True)  15.5 us
    ppermute x2, waiting for transfers between devices, shifted(): return lax.ppermute(block, SLAB, route)  13.1 us
    ppermute x2, starting transfers between devices, shifted(): return lax.ppermute(block, SLAB, route)  6.77 us
    pallas_call x1, Pallas kernels, forward(): pl.pallas_call(forward_kernel, out_shape=(jax.ShapeDtypeStruct((CELLS, OU...  4.53 us
    pallas_call x1, Pallas kernels, backward(): pl.pallas_call(backward_kernel, out_shape=jax.ShapeDtypeStruct((2, 2 * RO...  2.94 us
  transfers between devices with their start and end apart: 3, of which 3 were waited for; matrix products, arithmetic and copies ran while one was open for 0% of the time, Pallas kernels for 4%

profile of v2, /device:TPU:2, one launch (start us, length us, event | category | flops | bytes accessed | tf_op | source)
XLA Modules:
  0.0 83.9 jit_solution(4157550282402730511)
XLA Ops:
  0.6 0.9 %slice_bitcast_fusion = bf16[16,32,128]{2,1,0:T(8,128)(2,1)S(1)} fusion(bf16[1,2,16,32,128]{4,3,2,1,0:T(8,128)(2,1)} %param.3), kind=kLoop, calls=%fused_computation.1 | loop fusion | bytes 262144 | tf_op jit(solution)/shard_map/squeeze | solution.py:155
  1.5 3.4 %collective-permute-start = (bf16[16,32,128]{2,1,0:T(8,128)(2,1)S(1)}, bf16[16,32,128]{2,1,0:T(8,128)(2,1)S(1)}, u32[]{:S(2)}, u32[]{:S(2)}) collective-permute-start(bf16[16,32,128]{2,1,0:T(8,128)(2,1)S(1)} %slice_bitcast_fusion), channel_id=1, source_target_pairs={{0,1},{1,2},{2,3},{3,4},{4,5},{5,6},{6,7},{7,8},{8,9},{9,10},{10,1... | collective-permute-start | bytes 393224 | tf_op jit(solution)/shard_map/ppermute | solution.py:27
  5.0 10.3 %collective-permute-done.below_ref = bf16[16,32,128]{2,1,0:T(8,128)(2,1)S(1)} collective-permute-done((bf16[16,32,128]{2,1,0:T(8,128)(2,1)S(1)}, bf16[16,32,128]{2,1,0:T(8,128)(2,1)S(1)}, u32[]{:S(2)}, u32[]{:S(2)}) %collective-permute-start) | collective-permute-done | bytes 131104 | tf_op jit(solution)/shard_map/ppermute | solution.py:27
  15.3 0.0 copy-start
  15.3 0.7 copy-done
  15.9 4.5 %forward.1 = (bf16[128,256]{1,0:T(8,128)(2,1)}, bf16[128,256]{1,0:T(8,128)(2,1)}, bf16[2,4,6,144,128]{4,3,2,1,0:T(8,128)(2,1)}) custom-call(bf16[2,16,32,128]{3,2,1,0:T(8,128)(2,1)} %bitcast.20, bf16[16,32,128]{2,1,0:T(8,128)(2,1)} %copy-done, bf16[3456,256]{1,0:T(8,128)(2,1)} %bitcast.16, bf16[128,256]{1,0:T(8,128)(2,1)} %bitcast.23), custom_call_target="tpu_custom_call" | custom-call | flops 452984832 | bytes 4194304 | tf_op jit(solution)/shard_map/forward/pallas_call | solution.py:72
  20.5 6.3 %all_to_all.20 = bf16[2,4,6,144,128]{4,3,2,1,0:T(8,128)(2,1)S(1)} all-to-all(bf16[2,4,6,144,128]{4,3,2,1,0:T(8,128)(2,1)} %get-tuple-element.8), channel_id=1, replica_groups=mesh['y'=8,'zh'=2,'core'=2,'zl'=6,'x'=4] {'core'}, dimensions={0} | all-to-all | bytes 3538944 | tf_op jit(solution)/shard_map/all_to_all | solution.py:137
  26.8 0.4 reduce_sum.42
  27.2 15.3 %all_to_all.21 = bf16[4,6,144,128]{3,2,1,0:T(8,128)(2,1)S(1)} all-to-all(bf16[4,6,144,128]{3,2,1,0:T(8,128)(2,1)S(1)} %reduce_sum.42), channel_id=1, replica_groups=mesh['y'=8,'zh'=2,'core'=2,'zl'=6,'x'=4] {'x'}, dimensions={0} | all-to-all | bytes 1769472 | tf_op jit(solution)/shard_map/all_to_all | solution.py:137
  42.5 0.0 copy-start.1
  42.5 0.2 reduce_sum.43
  42.7 0.2 copy.9
  42.8 12.8 %all_to_all.22 = bf16[8,16,864]{2,1,0:T(8,128)(2,1)S(1)} all-to-all(bf16[8,16,864]{2,1,0:T(8,128)(2,1)S(1)} %bitcast.18), channel_id=1, replica_groups=mesh['y'=8,'zh'=2,'core'=2,'zl'=6,'x'=4] {'y'}, dimensions={0} | all-to-all | bytes 442368 | tf_op jit(solution)/shard_map/all_to_all | solution.py:137
  55.7 0.1 reshape.36
  55.8 0.7 copy.10
  56.5 15.5 %all-to-all-start.3 = ((f32[12,8,144]{2,1,0:T(8,128)}), f32[12,8,144]{2,1,0:T(8,128)S(1)}, u32[]{:S(2)}, u32[]{:S(2)}) async-start(f32[12,8,144]{2,1,0:T(8,128)} %bitcast.11), calls=%async_computation.3 | async-start | bytes 196608 | tf_op jit(solution)/shard_map/all_to_all | solution.py:137
  72.0 0.0 copy-done.1
  72.0 3.4 %collective-permute-start.1 = (bf16[128,256]{1,0:T(8,128)(2,1)S(1)}, bf16[128,256]{1,0:T(8,128)(2,1)S(1)}, u32[]{:S(2)}, u32[]{:S(2)}) collective-permute-start(bf16[128,256]{1,0:T(8,128)(2,1)S(1)} %copy-done.1), channel_id=1, source_target_pairs={{1,0},{2,1},{3,2},{4,3},{5,4},{6,5},{7,6},{8,7},{9,8},{10,9},{11,1... | collective-permute-start | bytes 196616 | tf_op jit(solution)/shard_map/ppermute | solution.py:27
  75.3 2.8 %collective-permute-done.1.next_ref = bf16[128,256]{1,0:T(8,128)(2,1)S(1)} collective-permute-done((bf16[128,256]{1,0:T(8,128)(2,1)S(1)}, bf16[128,256]{1,0:T(8,128)(2,1)S(1)}, u32[]{:S(2)}, u32[]{:S(2)}) %collective-permute-start.1) | collective-permute-done | bytes 65568 | tf_op jit(solution)/shard_map/ppermute | solution.py:27
  78.1 0.0 copy-start.2
  78.1 0.6 copy-done.2
  78.7 2.9 %backward.1 = bf16[2,16,32,128]{3,2,1,0:T(8,128)(2,1)} custom-call(bf16[128,256]{1,0:T(8,128)(2,1)} %get-tuple-element.7.grad_ref, bf16[128,256]{1,0:T(8,128)(2,1)} %copy-done.2, bf16[27,128,256]{2,1,0:T(8,128)(2,1)} %bitcast.17), custom_call_target="tpu_custom_call" | custom-call | flops 226492416 | bytes 3145728 | tf_op jit(solution)/shard_map/backward/pallas_call | solution.py:125
  81.7 1.6 %all-to-all-done.3 = f32[12,8,144]{2,1,0:T(8,128)S(1)} async-done(((f32[12,8,144]{2,1,0:T(8,128)}), f32[12,8,144]{2,1,0:T(8,128)S(1)}, u32[]{:S(2)}, u32[]{:S(2)}) %all-to-all-start.3) | async-done | bytes 55328 | tf_op jit(solution)/shard_map/all_to_all | solution.py:137
  83.3 0.6 multiply_bitcast_fusion
  (2 shorter events, 0.1 us)
Async XLA Ops:
  1.5 13.7 %collective-permute-start = (bf16[16,32,128]{2,1,0:T(8,128)(2,1)S(1)}, bf16[16,32,128]{2,1,0:T(8,128)(2,1)S(1)}, u32[]{:S(2)}, u32[]{:S(2)}) collective-permute-start(bf16[16,32,128]{2,1,0:T(8,128)(2,1)S(1)} %slice_bitcast_fusion), channel_id=1, source_target_pairs={{0,1},{1,2},{2,3},{3,4},{4,5},{5,6},{6,7},{7,8},{8,9},{9,10},{10,1... | collective-permute-start | bytes 393224 | tf_op jit(solution)/shard_map/ppermute | solution.py:27
  15.3 0.7 copy-start
  42.5 29.4 %copy-start.1 = (bf16[128,256]{1,0:T(8,128)(2,1)S(1)}, bf16[128,256]{1,0:T(8,128)(2,1)}, u32[]{:S(2)}) copy-start(bf16[128,256]{1,0:T(8,128)(2,1)} %get-tuple-element.7.grad_ref) | copy-start | bytes 196612
  56.5 26.8 %all-to-all-start.3 = ((f32[12,8,144]{2,1,0:T(8,128)}), f32[12,8,144]{2,1,0:T(8,128)S(1)}, u32[]{:S(2)}, u32[]{:S(2)}) async-start(f32[12,8,144]{2,1,0:T(8,128)} %bitcast.11), calls=%async_computation.3 | async-start | bytes 196608 | tf_op jit(solution)/shard_map/all_to_all | solution.py:137
  72.0 6.2 %collective-permute-start.1 = (bf16[128,256]{1,0:T(8,128)(2,1)S(1)}, bf16[128,256]{1,0:T(8,128)(2,1)S(1)}, u32[]{:S(2)}, u32[]{:S(2)}) collective-permute-start(bf16[128,256]{1,0:T(8,128)(2,1)S(1)} %copy-done.1), channel_id=1, source_target_pairs={{1,0},{2,1},{3,2},{4,3},{5,4},{6,5},{7,6},{8,7},{9,8},{10,9},{11,1... | collective-permute-start | bytes 196616 | tf_op jit(solution)/shard_map/ppermute | solution.py:27
  78.1 0.6 copy-start.2

commit v3 on v2

v3 whole, which is shorter than its diff:
```python
import math

import jax
import jax.numpy as jnp
from jax import lax
from jax.experimental import pallas as pl
from jax.experimental.pallas import tpu as pltpu
from jax.sharding import Mesh, PartitionSpec as P


Y, ZH, CORE, ZL, X = 8, 2, 2, 6, 4
AXES = ("y", "zh", "core", "zl", "x")
SLAB = ("zl", "x")
ROWS, COLS = 8, 16
IN, OUT = 128, 256
CELLS = ROWS * COLS
SHARE = 27 * IN // (ZL * X)
HALF = OUT // CORE
PAD = 8
GRANT = 12 << 20
BF, F32 = jnp.bfloat16, jnp.float32
VMEM = pl.BlockSpec(memory_space=pltpu.VMEM)


def shifted(block, distance):
    devices = range(ZL * X)
    route = [(i - distance, i) for i in devices if i - distance in devices]
    return lax.ppermute(block, SLAB, route)


def widen(wide, layer, h, source):
    wide[layer, h, 0:PAD, :] = jnp.zeros((PAD, IN), F32)
    wide[layer, h, PAD : PAD + 2 * COLS, :] = source.astype(F32)


def fill_patches(wide, layer, patches, first):
    for b in range(3):
        for c in range(3):
            lanes = slice((first + b * 3 + c) * IN, (first + b * 3 + c + 1) * IN)
            for p in range(ROWS):
                h = 2 * p - 1 + b
                if h < 0:
                    piece = jnp.zeros((COLS, IN), BF)
                else:
                    piece = wide[layer, h, pl.ds(PAD - 1 + c, COLS, stride=2), :].astype(BF)
                patches[p * COLS : (p + 1) * COLS, lanes] = piece


def own_kernel(low_ref, high_ref, weight_hbm, patches, pre_ref, weight_ref, wide, sem):
    copy = pltpu.make_async_copy(weight_hbm, weight_ref, sem)
    copy.start()
    for layer, source in enumerate((low_ref, high_ref)):
        for h in range(2 * ROWS):
            widen(wide, layer, h, source[h])
        fill_patches(wide, layer, patches, 9 * layer)
    copy.wait()
    pre_ref[...] = jnp.dot(patches[...], weight_ref[9 * IN :, :], preferred_element_type=F32)


def own_taps(low, high, weights):
    return pl.pallas_call(
        own_kernel,
        out_shape=(
            jax.ShapeDtypeStruct((CELLS, 18 * IN), BF),
            jax.ShapeDtypeStruct((CELLS, OUT), F32),
            jax.ShapeDtypeStruct((27 * IN, OUT), BF),
        ),
        in_specs=[VMEM] * 2 + [pl.BlockSpec(memory_space=pltpu.HBM)],
        out_specs=(VMEM,) * 3,
        scratch_shapes=[
            pltpu.VMEM((2, 2 * ROWS, PAD + 2 * COLS, IN), F32),
            pltpu.SemaphoreType.DMA(()),
        ],
        cost_estimate=pl.CostEstimate(flops=2 * CELLS * 18 * IN * OUT, bytes_accessed=3 << 20, transcendentals=0),
        compiler_params=pltpu.CompilerParams(vmem_limit_bytes=GRANT),
        name="own_taps",
    )(low, high, weights)


def weight_terms(patches, first, tap, grad, keep_ref, send_ref):
    lanes = slice((tap - first) * IN, (tap - first + 1) * IN)
    part = lax.dot_general(
        patches[:, lanes], grad, (((0,), (0,)), ((), ())), preferred_element_type=F32
    ).astype(BF)
    for k in range(IN // 16):
        slab, inner = divmod(tap * (IN // 16) + k, SHARE // 16)
        zl, x = divmod(slab, X)
        for half, ref in enumerate((keep_ref, send_ref)):
            ref[x, zl, inner * 16 : (inner + 1) * 16, :] = part[
                k * 16 : (k + 1) * 16, half * HALF : (half + 1) * HALF
            ]


def forward_kernel(
    me_ref, below_ref, weight_ref, own_patches, pre_ref, cot_ref, act_ref, grad_ref, keep_ref, send_ref, patches, wide
):
    for h in range(2 * ROWS):
        widen(wide, 0, h, below_ref[h])
    fill_patches(wide, 0, patches, 0)
    pre = pre_ref[...] + jnp.dot(patches[...], weight_ref[: 9 * IN, :], preferred_element_type=F32)
    sig = jax.nn.sigmoid(pre)
    act_ref[...] = (0.3 * pre + 0.7 * pre * sig).astype(BF)
    slope = 0.3 + 0.7 * (sig + pre * sig * (1.0 - sig))
    grad = (cot_ref[...].astype(F32) * slope).astype(BF)
    grad_ref[...] = grad
    me = me_ref[0]
    place = lax.broadcasted_iota(jnp.int32, (OUT, OUT), 1)
    origin = lax.broadcasted_iota(jnp.int32, (OUT, OUT), 0)
    who = jnp.where(place < HALF, me, 1 - me)
    wanted = (place % HALF) // 8 * 16 + who * 8 + place % 8
    choose = jnp.where(origin == wanted, 1.0, 0.0).astype(BF)
    ordered = jnp.dot(grad, choose, preferred_element_type=F32).astype(BF)
    for tap in range(27):
        held, first = (patches, 0) if tap < 9 else (own_patches, 9)
        weight_terms(held, first, tap, ordered, keep_ref, send_ref)


def forward(me, below, weights, own_patches, pre, cotangent):
    return pl.pallas_call(
        forward_kernel,
        out_shape=(
            jax.ShapeDtypeStruct((CELLS, OUT), BF),
            jax.ShapeDtypeStruct((CELLS, OUT), BF),
            jax.ShapeDtypeStruct((X, ZL, SHARE, HALF), BF),
            jax.ShapeDtypeStruct((X, ZL, SHARE, HALF), BF),
        ),
        in_specs=[pl.BlockSpec(memory_space=pltpu.SMEM)] + [VMEM] * 5,
        out_specs=(VMEM,) * 4,
        scratch_shapes=[
            pltpu.VMEM((CELLS, 9 * IN), BF),
            pltpu.VMEM((1, 2 * ROWS, PAD + 2 * COLS, IN), F32),
        ],
        cost_estimate=pl.CostEstimate(flops=3 * CELLS * 27 * IN * OUT, bytes_accessed=3 << 20, transcendentals=CELLS * OUT),
        compiler_params=pltpu.CompilerParams(vmem_limit_bytes=GRANT),
        name="forward",
    )(me, below, weights, own_patches, pre, cotangent)


def backward_kernel(grad_ref, next_ref, weight_ref, out_ref, wide):
    def moved(ref):
        grad = ref[...].astype(F32)
        cell = lax.broadcasted_iota(jnp.int32, (CELLS, OUT), 0)
        ahead = jnp.concatenate([grad[1:], jnp.zeros((1, OUT), F32)], axis=0)
        ahead = jnp.where(cell % COLS == COLS - 1, 0.0, ahead)
        blank = jnp.zeros((COLS, OUT), BF)
        found = {}
        for dq, value in ((0, ref[...]), (1, ahead.astype(BF))):
            found[0, dq] = value
            found[1, dq] = jnp.concatenate([value[COLS:], blank], axis=0)
        return found

    mine, after = moved(grad_ref), moved(next_ref)
    choices = {0: [(1, 0)], 1: [(2, 0), (0, 1)]}
    for layer in range(2):
        sources = [(1, mine)] if layer == 0 else [(2, mine), (0, after)]
        for hp in range(2):
            for wp in range(2):
                value = jnp.zeros((CELLS, IN), F32)
                for a, found in sources:
                    for b, dp in choices[hp]:
                        for c, dq in choices[wp]:
                            value += lax.dot_general(
                                found[dp, dq],
                                weight_ref[(a * 3 + b) * 3 + c],
                                (((1,), (1,)), ((), ())),
                                preferred_element_type=F32,
                            )
                for p in range(ROWS):
                    wide[layer, 2 * p + hp, pl.ds(wp, COLS, stride=2), :] = value[p * COLS : (p + 1) * COLS]
    out_ref[...] = wide[...].astype(BF)


def backward(grad, grad_next, weights):
    return pl.pallas_call(
        backward_kernel,
        out_shape=jax.ShapeDtypeStruct((2, 2 * ROWS, 2 * COLS, IN), BF),
        in_specs=[VMEM] * 3,
        out_specs=VMEM,
        scratch_shapes=[pltpu.VMEM((2, 2 * ROWS, 2 * COLS, IN), F32)],
        cost_estimate=pl.CostEstimate(flops=2 * CELLS * 27 * IN * OUT, bytes_accessed=3 << 20, transcendentals=0),
        compiler_params=pltpu.CompilerParams(vmem_limit_bytes=GRANT),
        name="backward",
    )(grad, grad_next, weights)


def exchange(block, axes):
    return lax.all_to_all(block, axes, 0, 0, tiled=True)


def total(parts):
    return jnp.sum(parts.astype(F32), axis=0)


def local(volumes, kernel, cotangent):
    low, high = volumes[0, 0], volumes[0, 1]
    below = shifted(high, 1)
    own_patches, pre, weights = own_taps(low, high, kernel.reshape(27 * IN, OUT))
    me = lax.axis_index("core").reshape(1)
    activation, out_grad, keep, send = forward(
        me, below, weights, own_patches, pre, cotangent.reshape(CELLS, OUT)
    )
    partner = lax.ppermute(send, "core", [(0, 1), (1, 0)])
    next_grad = shifted(out_grad, -1)
    grad = (keep.astype(F32) + partner.astype(F32)).astype(BF)
    grad = exchange(grad, "x")
    grad, out_grad = lax.optimization_barrier((grad, out_grad))
    input_grad = backward(out_grad, next_grad, weights.reshape(27, IN, OUT))
    grad, input_grad = lax.optimization_barrier((grad, input_grad))
    grad = total(grad).astype(BF)
    grad = grad.reshape(ZL * SHARE, HALF).T.reshape(Y, HALF // Y, ZL * SHARE)
    grad = total(exchange(grad, "y"))
    grad = grad.reshape(ZH, 8, ZL, SHARE).transpose(0, 2, 1, 3).reshape(ZH * ZL, 8, SHARE)
    grad = total(exchange(grad, ("zh", "zl"))).T
    norm_factor = 1.0 / math.sqrt(Y * ZH * CORE * ZL * X * CELLS)
    return (
        activation.reshape(1, 1, ROWS, COLS, OUT),
        input_grad[None],
        grad * norm_factor,
    )


def solution(mesh):
    fine = Mesh(mesh.devices.reshape(Y, ZH, CORE, ZL, X), AXES)
    split = P(("y", "zh", "core"), SLAB, None, None, None)
    out_specs = (split, split, P(SLAB, ("y", "zh", "core")))
    return jax.shard_map(local, mesh=fine, in_specs=(split, P(), split), out_specs=out_specs, check_vma=False)
```

time: 84.4 us -> 81.7 us (0.968)
  the two profiles are of different devices: /device:TPU:2 before, /device:TPU:6 now
where the time goes in v3:
time: 81.7 us; the launch traced here: 81.4 us
  blocking collectives  40.4 us (49%)
  starting transfers between devices  18.7 us (23%)
  waiting for transfers between devices  13.5 us (17%)
  Pallas kernels  3.34 us (4%)
  local copies, waits for them, and re-layouts  2.79 us (3%)
  other arithmetic  1.96 us (2%)
    all_to_all x2, blocking collectives, exchange(): return lax.all_to_all(block, axes, 0, 0, tiled=True)  40.4 us
    all_to_all x1, waiting for transfers between devices, exchange(): return lax.all_to_all(block, axes, 0, 0, tiled=True)  10.5 us
    all_to_all x1, starting transfers between devices, exchange(): return lax.all_to_all(block, axes, 0, 0, tiled=True)  9.84 us
    ppermute x2, starting transfers between devices, shifted(): return lax.ppermute(block, SLAB, route)  6.95 us
    ppermute x1, waiting for transfers between devices, local(): partner = lax.ppermute(send, 'core', [(0, 1), (1, 0)])  2.39 us
    ppermute x1, starting transfers between devices, local(): partner = lax.ppermute(send, 'core', [(0, 1), (1, 0)])  1.92 us
  transfers between devices with their start and end apart: 4, of which 3 were waited for; matrix products, arithmetic and copies ran while one was open for 0% of the time, Pallas kernels for 1%

profile of v3, /device:TPU:6, one launch (start us, length us, event | category | flops | bytes accessed | tf_op | source)
XLA Modules:
  0.0 81.4 jit_solution(2787915080565404703)
XLA Ops:
  0.6 0.0 copy-start.1
  0.6 1.0 %slice_bitcast_fusion = (bf16[16,32,128]{2,1,0:T(8,128)(2,1)S(1)}, bf16[16,32,128]{2,1,0:T(8,128)(2,1)S(1)}) fusion(bf16[1,2,16,32,128]{4,3,2,1,0:T(8,128)(2,1)} %param.3), kind=kLoop, calls=%fused_computation.2 | loop fusion | bytes 524288 | tf_op jit(solution)/shard_map/squeeze | solution.py:195
  1.7 4.2 %collective-permute-start = (bf16[16,32,128]{2,1,0:T(8,128)(2,1)S(1)}, bf16[16,32,128]{2,1,0:T(8,128)(2,1)S(1)}, u32[]{:S(2)}, u32[]{:S(2)}) collective-permute-start(bf16[16,32,128]{2,1,0:T(8,128)(2,1)S(1)} %get-tuple-element.26.high_ref), channel_id=1, source_target_pairs={{0,1},{1,2},{2,3},{3,4},{4,5},{5,6},{6,7},{7,8},{8,9},{9,10},{10,1... | collective-permute-start | bytes 393224 | tf_op jit(solution)/shard_map/ppermute | solution.py:28
  5.9 0.0 copy-start
  5.9 1.5 %copy-done = bf16[3,3,3,128,256]{4,3,2,1,0:T(8,128)(2,1)S(1)} copy-done((bf16[3,3,3,128,256]{4,3,2,1,0:T(8,128)(2,1)S(1)}, bf16[3,3,3,128,256]{4,3,2,1,0:T(8,128)(2,1)}, u32[]{:S(2)}) %copy-start) | copy-done | bytes 1769496
  7.3 0.8 %own_taps.1 = (bf16[128,2304]{1,0:T(8,128)(2,1)S(1)}, f32[128,256]{1,0:T(8,128)S(1)}, bf16[3456,256]{1,0:T(8,128)(2,1)S(1)}) custom-call(bf16[16,32,128]{2,1,0:T(8,128)(2,1)S(1)} %get-tuple-element.25.low_ref, bf16[16,32,128]{2,1,0:T(8,128)(2,1)S(1)} %get-tuple-element.26.high_ref, bf16[3456,256]{1,0:T(8,128)(2,1)S(1)} %bitcast.19), custom_call_target="tpu_custom_call" | custom-call | flops 150994944 | bytes 3145728 | tf_op jit(solution)/shard_map/own_taps/pallas_call | solution.py:61
  8.2 0.6 collective-permute-done.below_ref
  8.8 0.0 copy-done.1
  8.8 1.1 %forward.1 = (bf16[128,256]{1,0:T(8,128)(2,1)}, bf16[128,256]{1,0:T(8,128)(2,1)S(1)}, bf16[4,6,144,128]{3,2,1,0:T(8,128)(2,1)S(1)}, bf16[4,6,144,128]{3,2,1,0:T(8,128)(2,1)S(1)}) custom-call(s32[1]{0:T(128)} %bitcast.me_ref, bf16[16,32,128]{2,1,0:T(8,128)(2,1)S(1)} %collective-permute-done.below_ref, bf16[3456,256]{1,0:T(8,128)(2,1)S(1)} %get-tuple-element.14.weight_ref, ...), custom_call_target="tpu_custom_call" | custom-call | flops 339738624 | bytes 3145728 | tf_op jit(solution)/shard_map/forward/pallas_call | solution.py:119
  9.9 1.9 %collective-permute-start.1 = (bf16[4,6,144,128]{3,2,1,0:T(8,128)(2,1)S(1)}, bf16[4,6,144,128]{3,2,1,0:T(8,128)(2,1)S(1)}, u32[]{:S(2)}, u32[]{:S(2)}) collective-permute-start(bf16[4,6,144,128]{3,2,1,0:T(8,128)(2,1)S(1)} %get-tuple-element.19), channel_id=1, source_target_pairs={{0,24},{24,0},{1,25},{25,1},{2,26},{26,2},{3,27},{27,3},{4,28},{28... | collective-permute-start | bytes 2654216 | tf_op jit(solution)/shard_map/ppermute | solution.py:202
  11.9 2.4 %collective-permute-done.1 = bf16[4,6,144,128]{3,2,1,0:T(8,128)(2,1)S(1)} collective-permute-done((bf16[4,6,144,128]{3,2,1,0:T(8,128)(2,1)S(1)}, bf16[4,6,144,128]{3,2,1,0:T(8,128)(2,1)S(1)}, u32[]{:S(2)}, u32[]{:S(2)}) %collective-permute-start.1) | collective-permute-done | bytes 884768 | tf_op jit(solution)/shard_map/ppermute | solution.py:202
  14.2 1.1 %add_convert_fusion = bf16[4,6,144,128]{3,2,1,0:T(8,128)(2,1)} fusion(bf16[4,6,144,128]{3,2,1,0:T(8,128)(2,1)S(1)} %collective-permute-done.1, bf16[4,6,144,128]{3,2,1,0:T(8,128)(2,1)S(1)} %get-tuple-element.18), kind=kLoop, calls=%fused_computation | loop fusion | flops 1769472 | bytes 2654208 | tf_op jit(solution)/shard_map/convert_element_type | solution.py:204
  15.4 9.8 %all-to-all-start = ((bf16[4,6,144,128]{3,2,1,0:T(8,128)(2,1)}), bf16[4,6,144,128]{3,2,1,0:T(8,128)(2,1)S(1)}, u32[]{:S(2)}, u32[]{:S(2)}) async-start(bf16[4,6,144,128]{3,2,1,0:T(8,128)(2,1)} %add_convert_fusion), calls=%async_computation | async-start | bytes 1769472 | tf_op jit(solution)/shard_map/all_to_all | solution.py:187
  25.2 2.8 %collective-permute-start.2 = (bf16[128,256]{1,0:T(8,128)(2,1)S(1)}, bf16[128,256]{1,0:T(8,128)(2,1)S(1)}, u32[]{:S(2)}, u32[]{:S(2)}) collective-permute-start(bf16[128,256]{1,0:T(8,128)(2,1)S(1)} %get-tuple-element.22.grad_ref), channel_id=1, source_target_pairs={{1,0},{2,1},{3,2},{4,3},{5,4},{6,5},{7,6},{8,7},{9,8},{10,9},{11,1... | collective-permute-start | bytes 196616 | tf_op jit(solution)/shard_map/ppermute | solution.py:28
  28.0 10.5 %all-to-all-done = bf16[4,6,144,128]{3,2,1,0:T(8,128)(2,1)S(1)} async-done(((bf16[4,6,144,128]{3,2,1,0:T(8,128)(2,1)}), bf16[4,6,144,128]{3,2,1,0:T(8,128)(2,1)S(1)}, u32[]{:S(2)}, u32[]{:S(2)}) %all-to-all-start) | async-done | bytes 884768 | tf_op jit(solution)/shard_map/all_to_all | solution.py:187
  38.5 0.0 collective-permute-done.2.next_ref
  38.5 1.4 %backward.1 = bf16[2,16,32,128]{3,2,1,0:T(8,128)(2,1)} custom-call(bf16[128,256]{1,0:T(8,128)(2,1)S(1)} %get-tuple-element.22.grad_ref, bf16[128,256]{1,0:T(8,128)(2,1)S(1)} %collective-permute-done.2.next_ref, bf16[27,128,256]{2,1,0:T(8,128)(2,1)S(1)} %bitcast.18), custom_call_target="tpu_custom_call" | custom-call | flops 226492416 | bytes 3145728 | tf_op jit(solution)/shard_map/backward/pallas_call | solution.py:174
  39.9 0.2 reduce_sum.30
  40.0 0.2 copy.7
  40.2 13.0 %all_to_all.15 = bf16[8,16,864]{2,1,0:T(8,128)(2,1)S(1)} all-to-all(bf16[8,16,864]{2,1,0:T(8,128)(2,1)S(1)} %bitcast.21), channel_id=1, replica_groups=mesh['y'=8,'zh'=2,'core'=2,'zl'=6,'x'=4] {'y'}, dimensions={0} | all-to-all | bytes 442368 | tf_op jit(solution)/shard_map/all_to_all | solution.py:187
  53.3 0.1 reshape.40
  53.4 27.3 %all_to_all.16 = f32[12,8,144]{2,1,0:T(8,128)S(1)} all-to-all(f32[12,8,144]{2,1,0:T(8,128)S(1)} %bitcast.24), channel_id=1, replica_groups=mesh['y'=8,'zh'=2,'core'=2,'zl'=6,'x'=4] {'zh','zl'}, dimensions={0} | all-to-all | bytes 110592 | tf_op jit(solution)/shard_map/all_to_all | solution.py:187
  80.7 0.6 multiply_bitcast_fusion
  (3 shorter events, 0.1 us)
Async XLA Ops:
  0.6 8.2 %copy-start.1 = (bf16[1,1,8,16,256]{4,3,2,1,0:T(8,128)(2,1)S(1)}, bf16[1,1,8,16,256]{4,3,2,1,0:T(8,128)(2,1)}, u32[]{:S(2)}) copy-start(bf16[1,1,8,16,256]{4,3,2,1,0:T(8,128)(2,1)} %param.5) | copy-start | bytes 196612
  1.7 7.1 %collective-permute-start = (bf16[16,32,128]{2,1,0:T(8,128)(2,1)S(1)}, bf16[16,32,128]{2,1,0:T(8,128)(2,1)S(1)}, u32[]{:S(2)}, u32[]{:S(2)}) collective-permute-start(bf16[16,32,128]{2,1,0:T(8,128)(2,1)S(1)} %get-tuple-element.26.high_ref), channel_id=1, source_target_pairs={{0,1},{1,2},{2,3},{3,4},{4,5},{5,6},{6,7},{7,8},{8,9},{9,10},{10,1... | collective-permute-start | bytes 393224 | tf_op jit(solution)/shard_map/ppermute | solution.py:28
  5.9 1.5 %copy-start = (bf16[3,3,3,128,256]{4,3,2,1,0:T(8,128)(2,1)S(1)}, bf16[3,3,3,128,256]{4,3,2,1,0:T(8,128)(2,1)}, u32[]{:S(2)}) copy-start(bf16[3,3,3,128,256]{4,3,2,1,0:T(8,128)(2,1)} %param.4) | copy-start | bytes 5308420
  9.9 4.3 %collective-permute-start.1 = (bf16[4,6,144,128]{3,2,1,0:T(8,128)(2,1)S(1)}, bf16[4,6,144,128]{3,2,1,0:T(8,128)(2,1)S(1)}, u32[]{:S(2)}, u32[]{:S(2)}) collective-permute-start(bf16[4,6,144,128]{3,2,1,0:T(8,128)(2,1)S(1)} %get-tuple-element.19), channel_id=1, source_target_pairs={{0,24},{24,0},{1,25},{25,1},{2,26},{26,2},{3,27},{27,3},{4,28},{28... | collective-permute-start | bytes 2654216 | tf_op jit(solution)/shard_map/ppermute | solution.py:202
  15.4 23.1 %all-to-all-start = ((bf16[4,6,144,128]{3,2,1,0:T(8,128)(2,1)}), bf16[4,6,144,128]{3,2,1,0:T(8,128)(2,1)S(1)}, u32[]{:S(2)}, u32[]{:S(2)}) async-start(bf16[4,6,144,128]{3,2,1,0:T(8,128)(2,1)} %add_convert_fusion), calls=%async_computation | async-start | bytes 1769472 | tf_op jit(solution)/shard_map/all_to_all | solution.py:187
  25.2 13.2 %collective-permute-start.2 = (bf16[128,256]{1,0:T(8,128)(2,1)S(1)}, bf16[128,256]{1,0:T(8,128)(2,1)S(1)}, u32[]{:S(2)}, u32[]{:S(2)}) collective-permute-start(bf16[128,256]{1,0:T(8,128)(2,1)S(1)} %get-tuple-element.22.grad_ref), channel_id=1, source_target_pairs={{1,0},{2,1},{3,2},{4,3},{5,4},{6,5},{7,6},{8,7},{9,8},{10,9},{11,1... | collective-permute-start | bytes 196616 | tf_op jit(solution)/shard_map/ppermute | solution.py:28

commit v4 on v3

--- a/solution.py
+++ b/solution.py
@@ -203,12 +203,11 @@
     next_grad = shifted(out_grad, -1)
     grad = (keep.astype(F32) + partner.astype(F32)).astype(BF)
     grad = exchange(grad, "x")
-    grad, out_grad = lax.optimization_barrier((grad, out_grad))
-    input_grad = backward(out_grad, next_grad, weights.reshape(27, IN, OUT))
-    grad, input_grad = lax.optimization_barrier((grad, input_grad))
     grad = total(grad).astype(BF)
     grad = grad.reshape(ZL * SHARE, HALF).T.reshape(Y, HALF // Y, ZL * SHARE)
-    grad = total(exchange(grad, "y"))
+    grad, out_grad = lax.optimization_barrier((exchange(grad, "y"), out_grad))
+    input_grad = backward(out_grad, next_grad, weights.reshape(27, IN, OUT))
+    grad = total(grad)
     grad = grad.reshape(ZH, 8, ZL, SHARE).transpose(0, 2, 1, 3).reshape(ZH * ZL, 8, SHARE)
     grad = total(exchange(grad, ("zh", "zl"))).T
     norm_factor = 1.0 / math.sqrt(Y * ZH * CORE * ZL * X * CELLS)

time: 81.7 us -> 78.1 us (0.956)
  the two profiles are of different devices: /device:TPU:6 before, /device:TPU:2 now
where the time goes in v4:
time: 78.1 us; the launch traced here: 77.8 us
  blocking collectives  28.1 us (36%)
  starting transfers between devices  24.2 us (31%)
  waiting for transfers between devices  17 us (22%)
  local copies, waits for them, and re-layouts  3.41 us (4%)
  Pallas kernels  3.35 us (4%)
  other arithmetic  1.05 us (1%)
    all_to_all x2, blocking collectives, exchange(): return lax.all_to_all(block, axes, 0, 0, tiled=True)  28.1 us
    all_to_all x1, starting transfers between devices, exchange(): return lax.all_to_all(block, axes, 0, 0, tiled=True)  15.5 us
    ppermute x2, waiting for transfers between devices, shifted(): return lax.ppermute(block, SLAB, route)  10.8 us
    ppermute x2, starting transfers between devices, shifted(): return lax.ppermute(block, SLAB, route)  6.77 us
    all_to_all x1, waiting for transfers between devices, exchange(): return lax.all_to_all(block, axes, 0, 0, tiled=True)  3.78 us
    ppermute x1, waiting for transfers between devices, local(): partner = lax.ppermute(send, 'core', [(0, 1), (1, 0)])  2.39 us
    ppermute x1, starting transfers between devices, local(): partner = lax.ppermute(send, 'core', [(0, 1), (1, 0)])  1.92 us
  transfers between devices with their start and end apart: 4, of which 4 were waited for; matrix products, arithmetic and copies ran while one was open for 0% of the time, Pallas kernels for 3%

profile of v4, /device:TPU:2, one launch (start us, length us, event | category | flops | bytes accessed | tf_op | source)
XLA Modules:
  0.0 77.8 jit_solution(7183988526298334685)
XLA Ops:
  0.6 0.0 copy-start.1
  0.6 1.0 %slice_bitcast_fusion = (bf16[16,32,128]{2,1,0:T(8,128)(2,1)S(1)}, bf16[16,32,128]{2,1,0:T(8,128)(2,1)S(1)}) fusion(bf16[1,2,16,32,128]{4,3,2,1,0:T(8,128)(2,1)} %param.3), kind=kLoop, calls=%fused_computation.2 | loop fusion | bytes 524288 | tf_op jit(solution)/shard_map/squeeze | solution.py:195
  1.7 3.4 %collective-permute-start = (bf16[16,32,128]{2,1,0:T(8,128)(2,1)S(1)}, bf16[16,32,128]{2,1,0:T(8,128)(2,1)S(1)}, u32[]{:S(2)}, u32[]{:S(2)}) collective-permute-start(bf16[16,32,128]{2,1,0:T(8,128)(2,1)S(1)} %get-tuple-element.22.high_ref), channel_id=1, source_target_pairs={{0,1},{1,2},{2,3},{3,4},{4,5},{5,6},{6,7},{7,8},{8,9},{9,10},{10,1... | collective-permute-start | bytes 393224 | tf_op jit(solution)/shard_map/ppermute | solution.py:28
  5.1 0.0 copy-start
  5.1 1.5 %copy-done = bf16[3,3,3,128,256]{4,3,2,1,0:T(8,128)(2,1)S(1)} copy-done((bf16[3,3,3,128,256]{4,3,2,1,0:T(8,128)(2,1)S(1)}, bf16[3,3,3,128,256]{4,3,2,1,0:T(8,128)(2,1)}, u32[]{:S(2)}) %copy-start) | copy-done | bytes 1769496
  6.6 0.8 %own_taps.1 = (bf16[128,2304]{1,0:T(8,128)(2,1)S(1)}, f32[128,256]{1,0:T(8,128)S(1)}, bf16[3456,256]{1,0:T(8,128)(2,1)S(1)}) custom-call(bf16[16,32,128]{2,1,0:T(8,128)(2,1)S(1)} %get-tuple-element.21.low_ref, bf16[16,32,128]{2,1,0:T(8,128)(2,1)S(1)} %get-tuple-element.22.high_ref, bf16[3456,256]{1,0:T(8,128)(2,1)S(1)} %bitcast.19), custom_call_target="tpu_custom_call" | custom-call | flops 150994944 | bytes 3145728 | tf_op jit(solution)/shard_map/own_taps/pallas_call | solution.py:61
  7.4 8.0 %collective-permute-done.below_ref = bf16[16,32,128]{2,1,0:T(8,128)(2,1)S(1)} collective-permute-done((bf16[16,32,128]{2,1,0:T(8,128)(2,1)S(1)}, bf16[16,32,128]{2,1,0:T(8,128)(2,1)S(1)}, u32[]{:S(2)}, u32[]{:S(2)}) %collective-permute-start) | collective-permute-done | bytes 131104 | tf_op jit(solution)/shard_map/ppermute | solution.py:28
  15.4 0.0 copy-done.1
  15.4 1.1 %forward.1 = (bf16[128,256]{1,0:T(8,128)(2,1)}, bf16[128,256]{1,0:T(8,128)(2,1)S(1)}, bf16[4,6,144,128]{3,2,1,0:T(8,128)(2,1)S(1)}, bf16[4,6,144,128]{3,2,1,0:T(8,128)(2,1)S(1)}) custom-call(s32[1]{0:T(128)} %bitcast.me_ref, bf16[16,32,128]{2,1,0:T(8,128)(2,1)S(1)} %collective-permute-done.below_ref, bf16[3456,256]{1,0:T(8,128)(2,1)S(1)} %get-tuple-element.12.weight_ref, ...), custom_call_target="tpu_custom_call" | custom-call | flops 339738624 | bytes 3145728 | tf_op jit(solution)/shard_map/forward/pallas_call | solution.py:119
  16.5 1.9 %collective-permute-start.1 = (bf16[4,6,144,128]{3,2,1,0:T(8,128)(2,1)S(1)}, bf16[4,6,144,128]{3,2,1,0:T(8,128)(2,1)S(1)}, u32[]{:S(2)}, u32[]{:S(2)}) collective-permute-start(bf16[4,6,144,128]{3,2,1,0:T(8,128)(2,1)S(1)} %get-tuple-element.17), channel_id=1, source_target_pairs={{0,24},{24,0},{1,25},{25,1},{2,26},{26,2},{3,27},{27,3},{4,28},{28... | collective-permute-start | bytes 2654216 | tf_op jit(solution)/shard_map/ppermute | solution.py:202
  18.5 2.4 %collective-permute-done.1 = bf16[4,6,144,128]{3,2,1,0:T(8,128)(2,1)S(1)} collective-permute-done((bf16[4,6,144,128]{3,2,1,0:T(8,128)(2,1)S(1)}, bf16[4,6,144,128]{3,2,1,0:T(8,128)(2,1)S(1)}, u32[]{:S(2)}, u32[]{:S(2)}) %collective-permute-start.1) | collective-permute-done | bytes 884768 | tf_op jit(solution)/shard_map/ppermute | solution.py:202
  20.9 0.2 add_convert_fusion
  21.1 15.3 %all_to_all.15 = bf16[4,6,144,128]{3,2,1,0:T(8,128)(2,1)S(1)} all-to-all(bf16[4,6,144,128]{3,2,1,0:T(8,128)(2,1)S(1)} %add_convert_fusion), channel_id=1, replica_groups=mesh['y'=8,'zh'=2,'core'=2,'zl'=6,'x'=4] {'x'}, dimensions={0} | all-to-all | bytes 1769472 | tf_op jit(solution)/shard_map/all_to_all | solution.py:187
  36.4 0.2 reduce_sum.30
  36.5 0.2 copy.7
  36.7 12.8 %all_to_all.16 = bf16[8,16,864]{2,1,0:T(8,128)(2,1)S(1)} all-to-all(bf16[8,16,864]{2,1,0:T(8,128)(2,1)S(1)} %bitcast.21), channel_id=1, replica_groups=mesh['y'=8,'zh'=2,'core'=2,'zl'=6,'x'=4] {'y'}, dimensions={0} | all-to-all | bytes 442368 | tf_op jit(solution)/shard_map/all_to_all | solution.py:187
  49.6 0.1 reshape.40
  49.7 0.7 copy.8
  50.3 15.5 %all-to-all-start.2 = ((f32[12,8,144]{2,1,0:T(8,128)}), f32[12,8,144]{2,1,0:T(8,128)S(1)}, u32[]{:S(2)}, u32[]{:S(2)}) async-start(f32[12,8,144]{2,1,0:T(8,128)} %bitcast.12), calls=%async_computation.2 | async-start | bytes 196608 | tf_op jit(solution)/shard_map/all_to_all | solution.py:187
  65.8 3.4 %collective-permute-start.2 = (bf16[128,256]{1,0:T(8,128)(2,1)S(1)}, bf16[128,256]{1,0:T(8,128)(2,1)S(1)}, u32[]{:S(2)}, u32[]{:S(2)}) collective-permute-start(bf16[128,256]{1,0:T(8,128)(2,1)S(1)} %get-tuple-element.19.grad_ref), channel_id=1, source_target_pairs={{1,0},{2,1},{3,2},{4,3},{5,4},{6,5},{7,6},{8,7},{9,8},{10,9},{11,1... | collective-permute-start | bytes 196616 | tf_op jit(solution)/shard_map/ppermute | solution.py:28
  69.2 2.8 %collective-permute-done.2.next_ref = bf16[128,256]{1,0:T(8,128)(2,1)S(1)} collective-permute-done((bf16[128,256]{1,0:T(8,128)(2,1)S(1)}, bf16[128,256]{1,0:T(8,128)(2,1)S(1)}, u32[]{:S(2)}, u32[]{:S(2)}) %collective-permute-start.2) | collective-permute-done | bytes 65568 | tf_op jit(solution)/shard_map/ppermute | solution.py:28
  72.0 1.4 %backward.1 = bf16[2,16,32,128]{3,2,1,0:T(8,128)(2,1)} custom-call(bf16[128,256]{1,0:T(8,128)(2,1)S(1)} %get-tuple-element.19.grad_ref, bf16[128,256]{1,0:T(8,128)(2,1)S(1)} %collective-permute-done.2.next_ref, bf16[27,128,256]{2,1,0:T(8,128)(2,1)S(1)} %bitcast.18), custom_call_target="tpu_custom_call" | custom-call | flops 226492416 | bytes 3145728 | tf_op jit(solution)/shard_map/backward/pallas_call | solution.py:174
  73.4 3.8 %all-to-all-done.2 = f32[12,8,144]{2,1,0:T(8,128)S(1)} async-done(((f32[12,8,144]{2,1,0:T(8,128)}), f32[12,8,144]{2,1,0:T(8,128)S(1)}, u32[]{:S(2)}, u32[]{:S(2)}) %all-to-all-start.2) | async-done | bytes 55328 | tf_op jit(solution)/shard_map/all_to_all | solution.py:187
  77.2 0.6 multiply_bitcast_fusion
  (2 shorter events, 0.1 us)
Async XLA Ops:
  0.6 14.8 %copy-start.1 = (bf16[1,1,8,16,256]{4,3,2,1,0:T(8,128)(2,1)S(1)}, bf16[1,1,8,16,256]{4,3,2,1,0:T(8,128)(2,1)}, u32[]{:S(2)}) copy-start(bf16[1,1,8,16,256]{4,3,2,1,0:T(8,128)(2,1)} %param.5) | copy-start | bytes 196612
  1.7 13.7 %collective-permute-start = (bf16[16,32,128]{2,1,0:T(8,128)(2,1)S(1)}, bf16[16,32,128]{2,1,0:T(8,128)(2,1)S(1)}, u32[]{:S(2)}, u32[]{:S(2)}) collective-permute-start(bf16[16,32,128]{2,1,0:T(8,128)(2,1)S(1)} %get-tuple-element.22.high_ref), channel_id=1, source_target_pairs={{0,1},{1,2},{2,3},{3,4},{4,5},{5,6},{6,7},{7,8},{8,9},{9,10},{10,1... | collective-permute-start | bytes 393224 | tf_op jit(solution)/shard_map/ppermute | solution.py:28
  5.1 1.5 %copy-start = (bf16[3,3,3,128,256]{4,3,2,1,0:T(8,128)(2,1)S(1)}, bf16[3,3,3,128,256]{4,3,2,1,0:T(8,128)(2,1)}, u32[]{:S(2)}) copy-start(bf16[3,3,3,128,256]{4,3,2,1,0:T(8,128)(2,1)} %param.4) | copy-start | bytes 5308420
  16.5 4.3 %collective-permute-start.1 = (bf16[4,6,144,128]{3,2,1,0:T(8,128)(2,1)S(1)}, bf16[4,6,144,128]{3,2,1,0:T(8,128)(2,1)S(1)}, u32[]{:S(2)}, u32[]{:S(2)}) collective-permute-start(bf16[4,6,144,128]{3,2,1,0:T(8,128)(2,1)S(1)} %get-tuple-element.17), channel_id=1, source_target_pairs={{0,24},{24,0},{1,25},{25,1},{2,26},{26,2},{3,27},{27,3},{4,28},{28... | collective-permute-start | bytes 2654216 | tf_op jit(solution)/shard_map/ppermute | solution.py:202
  50.3 26.8 %all-to-all-start.2 = ((f32[12,8,144]{2,1,0:T(8,128)}), f32[12,8,144]{2,1,0:T(8,128)S(1)}, u32[]{:S(2)}, u32[]{:S(2)}) async-start(f32[12,8,144]{2,1,0:T(8,128)} %bitcast.12), calls=%async_computation.2 | async-start | bytes 196608 | tf_op jit(solution)/shard_map/all_to_all | solution.py:187
  65.8 6.2 %collective-permute-start.2 = (bf16[128,256]{1,0:T(8,128)(2,1)S(1)}, bf16[128,256]{1,0:T(8,128)(2,1)S(1)}, u32[]{:S(2)}, u32[]{:S(2)}) collective-permute-start(bf16[128,256]{1,0:T(8,128)(2,1)S(1)} %get-tuple-element.19.grad_ref), channel_id=1, source_target_pairs={{1,0},{2,1},{3,2},{4,3},{5,4},{6,5},{7,6},{8,7},{9,8},{10,9},{11,1... | collective-permute-start | bytes 196616 | tf_op jit(solution)/shard_map/ppermute | solution.py:28
